TPU v7x, 32 devices: a whole 2x2x4 slice. The times are simulated.
32 devices in a mesh: row: 8 (over y, x, core), col: 4 (over z).
Axes of the slice: x: 2, y: 2, z: 4, core: 2. Of those that a mesh axis runs over, the one named last changes fastest.
Arguments:
- left_act: bfloat16 [32, 64, 256], P(None, 'col', 'row'), may hold values from -6 to 6
- right_act: bfloat16 [32, 64, 256], P(None, 'row', 'col'), may hold values from -6 to 6
- cotangent: bfloat16 [256, 256, 128], P('row', 'col'), may hold values from -4 to 4
- weight: bfloat16 [1024, 128], replicated, may hold values from -0.1875 to 0.1875
Outputs:
- grad_left: float32 [32, 64, 256], P(None, 'col', 'row')
- grad_right: float32 [32, 64, 256], P(None, 'row', 'col')
- grad_weight: float32 [1024, 128], P('row')
All inputs are finite; a program needn't handle non-finite values.
Results may differ from a plain program's by a relative error of at most 0.0029.
Values may be sent and summed in bfloat16 or wider, within the bound.
No kernel may reach another device: no remote copies, remote signals or barrier semaphores. Data moves between devices by JAX's collectives and lax.ppermute only.
A program may use at most 128 MiB of HBM per device.

v0:
```python
import jax
import jax.numpy as jnp
from jax import lax
from jax.sharding import PartitionSpec as P

S = 64


def body(left_act, right_act, cotangent, weight):
    left = lax.all_gather(left_act, "col", axis=1, tiled=True)
    right = lax.all_gather(right_act, "row", axis=1, tiled=True)
    first, second = (cotangent.shape[0], cotangent.shape[1])
    chans = left.shape[0]
    outer = (
        jnp.einsum("csi,dsj->ijcd", left, right, preferred_element_type=jnp.float32) / S
    ).astype(jnp.bfloat16)
    outer_flat = outer.reshape(first * second, chans * chans)
    grad_flat = cotangent.reshape(first * second, cotangent.shape[2])
    contract = (((0,), (0,)), ((), ()))
    partial_w = lax.dot_general(outer_flat, grad_flat, contract, preferred_element_type=jnp.float32)
    own_rows = lax.psum_scatter(partial_w, "row", scatter_dimension=0, tiled=True)
    grad_weight = lax.psum(own_rows, "col")
    grad_outer = lax.dot_general(
        grad_flat, weight, (((1,), (1,)), ((), ())), preferred_element_type=jnp.float32
    )
    grad_outer = grad_outer.astype(jnp.bfloat16).reshape(first, second, chans, chans)
    left_part = (
        jnp.einsum("ijcd,dsj->csi", grad_outer, right, preferred_element_type=jnp.float32) / S
    )
    right_part = (
        jnp.einsum("ijcd,csi->dsj", grad_outer, left, preferred_element_type=jnp.float32) / S
    )
    grad_left = lax.psum_scatter(left_part, "col", scatter_dimension=1, tiled=True)
    grad_right = lax.psum_scatter(right_part, "row", scatter_dimension=1, tiled=True)
    return (grad_left, grad_right, grad_weight)


def solution(mesh):
    return jax.shard_map(
        body,
        mesh=mesh,
        in_specs=(P(None, "col", "row"), P(None, "row", "col"), P("row", "col", None), P()),
        out_specs=(P(None, "col", "row"), P(None, "row", "col"), P("row", None)),
        check_vma=False,
    )
```

profile of v0, /device:TPU:0, one launch (start us, length us, event | category | flops | bytes accessed | tf_op | source)
XLA Modules:
  0.0 213.5 jit_solution(4263041880610660756)
XLA Ops:
  7.2 0.0 reduce-scatter.8.cloned.1.call-start
  7.2 17.7 %all_gather.7 = bf16[32,64,32]{2,1,0:T(8,128)(2,1)S(1)} all-gather(bf16[32,16,32]{2,1,0:T(8,128)(2,1)} %param.4), channel_id=1, replica_groups=mesh['row'=8,'col'=4] {'col'}, dimensions={1}, use_global_device_ids=true | all-gather | bytes 163840 | tf_op jit(solution)/shard_map/all_gather | solution.py:10
  24.9 10.3 %all_gather.6 = bf16[32,64,64]{2,1,0:T(8,128)(2,1)S(1)} all-gather(bf16[32,8,64]{2,1,0:T(8,128)(2,1)} %param.5), channel_id=1, replica_groups=mesh['row'=8,'col'=4] {'row'}, dimensions={1}, use_global_device_ids=true | all-gather | bytes 294912 | tf_op jit(solution)/shard_map/all_gather | solution.py:11
  35.2 5.6 %fusion = bf16[32,64,32,32]{1,0,2,3:T(8,128)(2,1)} fusion(bf16[32,64,64]{2,1,0:T(8,128)(2,1)S(1)} %all_gather.6, bf16[32,64,32]{2,1,0:T(8,128)(2,1)S(1)} %all_gather.7), kind=kOutput, calls=%fused_computation.1 | convolution fusion | flops 272629760 | bytes 4587520 | tf_op jit(solution)/shard_map/csi,dsj->ijcd/dot_general | solution.py:15
  40.8 9.1 %copy.20 = bf16[32,64,32,32]{1,0,3,2:T(8,128)(2,1)} copy(bf16[32,64,32,32]{1,0,2,3:T(8,128)(2,1)} %fusion) | data formatting | bytes 8388608 | tf_op jit(solution)/shard_map/convert_element_type | solution.py:16
  49.9 12.4 %reshape.17 = bf16[2048,1024]{0,1:T(8,128)(2,1)} reshape(bf16[32,64,32,32]{1,0,3,2:T(8,128)(2,1)} %copy.20) | data formatting | bytes 8388608 | tf_op jit(solution)/shard_map/reshape | solution.py:17
  62.3 4.3 %fusion.9 = f32[1024,128]{1,0:T(8,128)} fusion(bf16[2048,1024]{0,1:T(8,128)(2,1)} %reshape.17, bf16[2048,128]{1,0:T(8,128)(2,1)S(1)} %bitcast.47), kind=kOutput, calls=%fused_computation.13 | convolution fusion | flops 536870912 | bytes 5242880 | tf_op jit(solution)/shard_map/dot_general | solution.py:20
  66.6 0.0 reduce-scatter.4.cloned.1.call-start
  66.7 3.2 %convolution_convert_fusion = bf16[2048,1024]{1,0:T(8,128)(2,1)} fusion(bf16[2048,128]{1,0:T(8,128)(2,1)S(1)} %bitcast.46, bf16[1024,128]{1,0:T(8,128)(2,1)S(1)} %copy-done.1), kind=kOutput, calls=%fused_computation.2 | convolution fusion | flops 538968064 | bytes 4980736 | tf_op jit(solution)/shard_map/dot_general | solution.py:23
  69.8 6.5 %copy.17 = bf16[2048,1024]{0,1:T(8,128)(2,1)} copy(bf16[2048,1024]{1,0:T(8,128)(2,1)} %convolution_convert_fusion) | data formatting | bytes 8388608 | tf_op jit(solution)/shard_map/convert_element_type | solution.py:26
  76.3 12.9 %reshape.16 = bf16[32,64,32,32]{1,0,3,2:T(8,128)(2,1)} reshape(bf16[2048,1024]{0,1:T(8,128)(2,1)} %copy.17) | data formatting | bytes 8388608 | tf_op jit(solution)/shard_map/reshape | solution.py:26
  89.2 5.7 %fusion.4 = f32[32,64,32]{1,2,0:T(8,128)S(1)} fusion(bf16[32,64,32,32]{1,0,3,2:T(8,128)(2,1)} %reshape.16, bf16[32,64,64]{2,1,0:T(8,128)(2,1)S(1)} %all_gather.6), kind=kOutput, calls=%fused_computation.8 | convolution fusion | flops 268500992 | bytes 4718592 | tf_op jit(solution)/shard_map/ijcd,dsj->csi/dot_general | solution.py:28
  95.0 1.8 copy.18
  96.8 0.2 reduce-scatter.6.cloned.1.call-start
  97.1 7.0 %fusion.2 = f32[32,64,64]{1,2,0:T(8,128)S(1)} fusion(bf16[32,64,32,32]{1,0,3,2:T(8,128)(2,1)} %reshape.16, bf16[32,64,32]{2,1,0:T(8,128)(2,1)S(1)} %all_gather.7), kind=kOutput, calls=%fused_computation.5 | convolution fusion | flops 268566528 | bytes 4849664 | tf_op jit(solution)/shard_map/ijcd,csi->dsj/dot_general | solution.py:31
  104.1 1.8 copy.19
  105.9 0.0 all-reduce.2.cloned.1.call-start
  106.0 0.5 all-reduce.2.cloned.1.call-update
  106.5 24.8 %reduce-scatter.4.cloned.1.call-done = f32[32,16,32]{2,0,1:T(8,128)} async-done(((f32[32,64,32]{2,0,1:T(8,128)}), f32[32,16,32]{2,0,1:T(8,128)}) %reduce-scatter.4.cloned.1.call-update) | async-done | bytes 65552 | tf_op jit(solution)/shard_map/reduce_scatter | solution.py:33
  131.3 1.8 copy.21
  133.1 35.9 %reduce-scatter.6.cloned.1.call-done = f32[32,8,64]{2,0,1:T(8,128)} async-done(((f32[32,64,64]{2,0,1:T(8,128)}), f32[32,8,64]{2,0,1:T(8,128)}) %reduce-scatter.6.cloned.1.call-update) | async-done | bytes 65552 | tf_op jit(solution)/shard_map/reduce_scatter | solution.py:34
  169.0 1.6 copy.22
  170.6 34.9 %all-reduce.2.cloned.1.call-done = f32[128,128]{1,0:T(8,128)} async-done(((f32[128,128]{1,0:T(8,128)}), f32[128,128]{1,0:T(8,128)}) %all-reduce.2.cloned.1.call-update) | async-done | bytes 65552 | tf_op jit(solution)/shard_map/psum | solution.py:22
  205.5 1.5 copy.27
  (8 shorter events, 0.1 us)
Async XLA Ops:
  7.2 55.2 %copy-start = (bf16[32,64,128]{2,1,0:T(8,128)(2,1)S(1)}, bf16[32,64,128]{2,1,0:T(8,128)(2,1)}, u32[]{:S(2)}) copy-start(bf16[32,64,128]{2,1,0:T(8,128)(2,1)} %param.6) | copy-start | bytes 1572868
  7.2 98.8 %reduce-scatter.8.cloned.1.call-start = ((), (), s32[]{:S(2)}) async-start(), calls=%async_computation.5 | async-start | bytes 589824 | tf_op jit(solution)/shard_map/reduce_scatter | solution.py:21
  49.9 16.7 %copy-start.1 = (bf16[1024,128]{1,0:T(8,128)(2,1)S(1)}, bf16[1024,128]{1,0:T(8,128)(2,1)}, u32[]{:S(2)}) copy-start(bf16[1024,128]{1,0:T(8,128)(2,1)} %param.7) | copy-start | bytes 786436
  66.6 64.7 %reduce-scatter.4.cloned.1.call-start = ((), (), s32[]{:S(2)}) async-start(), calls=%async_computation.3 | async-start | bytes 1310720 | tf_op jit(solution)/shard_map/reduce_scatter | solution.py:33
  96.8 72.1 %reduce-scatter.6.cloned.1.call-start = ((), (), s32[]{:S(2)}) async-start(), calls=%async_computation.4 | async-start | bytes 1179648 | tf_op jit(solution)/shard_map/reduce_scatter | solution.py:34
  105.9 99.6 %all-reduce.2.cloned.1.call-start = ((), (), s32[]{:S(2)}) async-start(), calls=%async_computation.6 | async-start | bytes 131072 | tf_op jit(solution)/shard_map/psum | solution.py:22
Sparse Core Ops, SparseCore 0:
  66.7 34.8 reduce-scatter.7
  103.9 27.3 reduce-scatter.3
  134.5 34.4 reduce-scatter.5
  171.1 34.2 all-reduce.1
where the time goes:
time: 215 us; the launch traced here: 213 us
  waiting for transfers between devices  96.1 us (45%)
  local copies, waits for them, and re-layouts  49.4 us (23%)
  blocking collectives  28 us (13%)
  matrix products  25.8 us (12%)
  between operations  13.8 us (6%)
    reduce_scatter x1, waiting for transfers between devices, body(): lax.psum_scatter(right_part, 'row', scatter_dimension=1, tiled=True)  35.9 us
    psum x1, waiting for transfers between devices, body(): grad_weight = lax.psum(own_rows, 'col')  34.9 us
    reduce_scatter x1, waiting for transfers between devices, body(): lax.psum_scatter(left_part, 'col', scatter_dimension=1, tiled=True)  24.8 us
    all_gather x1, blocking collectives, body(): left = lax.all_gather(left_act, 'col', axis=1, tiled=True)  17.7 us
    reshape x1, local copies, waits for them, and re-layouts, body(): grad_outer.astype(jnp.bfloat16).reshape(first, second, chans, chans)  12.9 us
    reshape x1, local copies, waits for them, and re-layouts, body(): outer_flat = outer.reshape(first * second, chans * chans)  12.4 us
    all_gather x1, blocking collectives, body(): right = lax.all_gather(right_act, 'row', axis=1, tiled=True)  10.3 us
    convert_element_type x1, local copies, waits for them, and re-layouts, body(): outer = (jnp.einsum('csi,dsj->ijcd', left, right, preferred_element_type=...  9.13 us
  transfers between devices with their start and end apart: 4, of which 3 were waited for; matrix products, arithmetic and copies ran while one was open for 20% of the time, Pallas kernels for 0%

commit v1 on v0

--- a/solution.py
+++ b/solution.py
@@ -7,7 +7,9 @@
 
 
 def body(left_act, right_act, cotangent, weight):
-    left = lax.all_gather(left_act, "col", axis=1, tiled=True)
+    left = jnp.concatenate(
+        lax.all_to_all(jnp.stack([left_act] * lax.axis_size("col")), "col", 0, 0), axis=1
+    )
     right = lax.all_gather(right_act, "row", axis=1, tiled=True)
     first, second = (cotangent.shape[0], cotangent.shape[1])
     chans = left.shape[0]

time: 215 us -> 205 us (0.953)
  blocking collectives: 28 us -> 10.3 us
  starting transfers between devices: 0.34 us -> 6.65 us
  local copies, waits for them, and re-layouts: 49.4 us -> 51.9 us
    all_gather x1 -> x0, blocking collectives: 17.7 us -> none  [body(): left = lax.all_gather(left_act, 'col', axis=1, tiled=True)]
    all_to_all x0 -> x1, starting transfers between devices: none -> 6.35 us  [body(): lax.all_to_all(jnp.stack([left_act] * lax.axis_size('col')), 'col', 0, 0)]
    unnamed x7 -> x9, local copies, waits for them, and re-layouts: 4.93 us -> 6.36 us
  transfers between devices with their start and end apart: 4 -> 5, of which waited for: 3 -> 3; matrix products, arithmetic and copies ran while one was open for 20% -> 21% of each run, Pallas kernels for 0% -> 0%
where the time goes in v1:
time: 205 us; the launch traced here: 204 us
  waiting for transfers between devices  95.8 us (47%)
  local copies, waits for them, and re-layouts  51.9 us (25%)
  matrix products  25.8 us (13%)
  between operations  13.8 us (7%)
  blocking collectives  10.3 us (5%)
  starting transfers between devices  6.65 us (3%)
    reduce_scatter x1, waiting for transfers between devices, body(): lax.psum_scatter(right_part, 'row', scatter_dimension=1, tiled=True)  35.9 us
    psum x1, waiting for transfers between devices, body(): grad_weight = lax.psum(own_rows, 'col')  34.8 us
    reduce_scatter x1, waiting for transfers between devices, body(): lax.psum_scatter(left_part, 'col', scatter_dimension=1, tiled=True)  24.5 us
    reshape x1, local copies, waits for them, and re-layouts, body(): grad_outer.astype(jnp.bfloat16).reshape(first, second, chans, chans)  12.9 us
    reshape x1, local copies, waits for them, and re-layouts, body(): outer_flat = outer.reshape(first * second, chans * chans)  12.4 us
    all_gather x1, blocking collectives, body(): right = lax.all_gather(right_act, 'row', axis=1, tiled=True)  10.3 us
    convert_element_type x1, local copies, waits for them, and re-layouts, body(): outer = (jnp.einsum('csi,dsj->ijcd', left, right, preferred_element_type=...  9.12 us
    dot_general x1, matrix products, body(): jnp.einsum('ijcd,csi->dsj', grad_outer, left, preferred_element_type=jnp....  7.02 us
  transfers between devices with their start and end apart: 5, of which 3 were waited for; matrix products, arithmetic and copies ran while one was open for 21% of the time, Pallas kernels for 0%

profile of v1, /device:TPU:0, one launch (start us, length us, event | category | flops | bytes accessed | tf_op | source)
XLA Modules:
  0.0 204.3 jit_solution(16011743856938152748)
XLA Ops:
  7.2 1.0 stack.2
  8.2 1.2 reshape.33
  9.4 6.3 %all-to-all-start = ((bf16[4,2,8192]{2,1,0:T(2,128)(2,1)}), bf16[4,2,8192]{2,1,0:T(2,128)(2,1)S(1)}, u32[]{:S(2)}, u32[]{:S(2)}) async-start(bf16[4,2,8192]{2,1,0:T(2,128)(2,1)} %reshape.33), calls=%async_computation.1 | async-start | bytes 262144 | tf_op jit(solution)/shard_map/all_to_all | solution.py:11
  15.7 10.3 %all_gather.3 = bf16[32,64,64]{2,1,0:T(8,128)(2,1)S(1)} all-gather(bf16[32,8,64]{2,1,0:T(8,128)(2,1)} %param.5), channel_id=1, replica_groups=mesh['row'=8,'col'=4] {'row'}, dimensions={1}, use_global_device_ids=true | all-gather | bytes 294912 | tf_op jit(solution)/shard_map/all_gather | solution.py:13
  26.0 0.3 reshape.34
  26.3 5.6 %fusion = bf16[32,64,32,32]{1,0,2,3:T(8,128)(2,1)} fusion(bf16[32,64,32,1]{2,1,0,3:T(8,128)(2,1)S(1)} %bitcast.50, bf16[32,64,64]{2,1,0:T(8,128)(2,1)S(1)} %all_gather.3), kind=kOutput, calls=%fused_computation.1 | convolution fusion | flops 272629760 | bytes 4587520 | tf_op jit(solution)/shard_map/csi,dsj->ijcd/dot_general | solution.py:17
  31.9 9.1 %copy.26 = bf16[32,64,32,32]{1,0,3,2:T(8,128)(2,1)} copy(bf16[32,64,32,32]{1,0,2,3:T(8,128)(2,1)} %fusion) | data formatting | bytes 8388608 | tf_op jit(solution)/shard_map/convert_element_type | solution.py:18
  41.0 12.4 %reshape.27 = bf16[2048,1024]{0,1:T(8,128)(2,1)} reshape(bf16[32,64,32,32]{1,0,3,2:T(8,128)(2,1)} %copy.26) | data formatting | bytes 8388608 | tf_op jit(solution)/shard_map/reshape | solution.py:19
  53.4 4.2 %fusion.7 = f32[1024,128]{1,0:T(8,128)} fusion(bf16[2048,1024]{0,1:T(8,128)(2,1)} %reshape.27, bf16[2048,128]{1,0:T(8,128)(2,1)S(1)} %bitcast.49), kind=kOutput, calls=%fused_computation.11 | convolution fusion | flops 536870912 | bytes 5242880 | tf_op jit(solution)/shard_map/dot_general | solution.py:22
  57.7 0.2 reduce-scatter.4.cloned.1.call-start
  57.9 3.2 %convolution_convert_fusion = bf16[2048,1024]{1,0:T(8,128)(2,1)} fusion(bf16[2048,128]{1,0:T(8,128)(2,1)S(1)} %bitcast.48, bf16[1024,128]{1,0:T(8,128)(2,1)S(1)} %copy-done.1), kind=kOutput, calls=%fused_computation.2 | convolution fusion | flops 538968064 | bytes 4980736 | tf_op jit(solution)/shard_map/dot_general | solution.py:25
  61.1 6.5 %copy.20 = bf16[2048,1024]{0,1:T(8,128)(2,1)} copy(bf16[2048,1024]{1,0:T(8,128)(2,1)} %convolution_convert_fusion) | data formatting | bytes 8388608 | tf_op jit(solution)/shard_map/convert_element_type | solution.py:28
  67.6 12.9 %reshape.24 = bf16[32,64,32,32]{1,0,3,2:T(8,128)(2,1)} reshape(bf16[2048,1024]{0,1:T(8,128)(2,1)} %copy.20) | data formatting | bytes 8388608 | tf_op jit(solution)/shard_map/reshape | solution.py:28
  80.5 5.7 %fusion.4 = f32[32,64,32]{1,2,0:T(8,128)S(1)} fusion(bf16[32,64,32,32]{1,0,3,2:T(8,128)(2,1)} %reshape.24, bf16[32,64,64]{2,1,0:T(8,128)(2,1)S(1)} %all_gather.3), kind=kOutput, calls=%fused_computation.8 | convolution fusion | flops 268500992 | bytes 4718592 | tf_op jit(solution)/shard_map/ijcd,dsj->csi/dot_general | solution.py:30
  86.3 1.8 copy.21
  88.2 7.0 %fusion.2 = f32[32,64,64]{1,2,0:T(8,128)S(1)} fusion(bf16[32,64,32,32]{1,0,3,2:T(8,128)(2,1)} %reshape.24, bf16[32,64,32,1]{2,1,3,0:T(8,128)(2,1)S(1)} %bitcast.51), kind=kOutput, calls=%fused_computation.5 | convolution fusion | flops 268566528 | bytes 4849664 | tf_op jit(solution)/shard_map/ijcd,csi->dsj/dot_general | solution.py:33
  95.2 1.7 copy.24
  97.1 0.5 all-reduce.2.cloned.1.call-update
  97.6 24.5 %reduce-scatter.4.cloned.1.call-done = f32[32,16,32]{2,0,1:T(8,128)} async-done(((f32[32,64,32]{2,0,1:T(8,128)}), f32[32,16,32]{2,0,1:T(8,128)}) %reduce-scatter.4.cloned.1.call-update) | async-done | bytes 65552 | tf_op jit(solution)/shard_map/reduce_scatter | solution.py:35
  122.1 1.8 copy.27
  123.9 35.9 %reduce-scatter.6.cloned.1.call-done = f32[32,8,64]{2,0,1:T(8,128)} async-done(((f32[32,64,64]{2,0,1:T(8,128)}), f32[32,8,64]{2,0,1:T(8,128)}) %reduce-scatter.6.cloned.1.call-update) | async-done | bytes 65552 | tf_op jit(solution)/shard_map/reduce_scatter | solution.py:36
  159.8 1.6 copy.28
  161.4 34.8 %all-reduce.2.cloned.1.call-done = f32[128,128]{1,0:T(8,128)} async-done(((f32[128,128]{1,0:T(8,128)}), f32[128,128]{1,0:T(8,128)}) %all-reduce.2.cloned.1.call-update) | async-done | bytes 65552 | tf_op jit(solution)/shard_map/psum | solution.py:24
  196.3 1.5 copy.37
  (13 shorter events, 0.2 us)
Async XLA Ops:
  7.2 46.3 %copy-start = (bf16[32,64,128]{2,1,0:T(8,128)(2,1)S(1)}, bf16[32,64,128]{2,1,0:T(8,128)(2,1)}, u32[]{:S(2)}) copy-start(bf16[32,64,128]{2,1,0:T(8,128)(2,1)} %param.6) | copy-start | bytes 1572868
  9.4 16.6 %all-to-all-start = ((bf16[4,2,8192]{2,1,0:T(2,128)(2,1)}), bf16[4,2,8192]{2,1,0:T(2,128)(2,1)S(1)}, u32[]{:S(2)}, u32[]{:S(2)}) async-start(bf16[4,2,8192]{2,1,0:T(2,128)(2,1)} %reshape.33), calls=%async_computation.1 | async-start | bytes 262144 | tf_op jit(solution)/shard_map/all_to_all | solution.py:11
  15.7 81.3 %reduce-scatter.8.cloned.1.call-start = ((), (), s32[]{:S(2)}) async-start(), calls=%async_computation.6 | async-start | bytes 589824 | tf_op jit(solution)/shard_map/reduce_scatter | solution.py:23
  41.0 16.9 %copy-start.1 = (bf16[1024,128]{1,0:T(8,128)(2,1)S(1)}, bf16[1024,128]{1,0:T(8,128)(2,1)}, u32[]{:S(2)}) copy-start(bf16[1024,128]{1,0:T(8,128)(2,1)} %param.7) | copy-start | bytes 786436
  57.7 64.4 %reduce-scatter.4.cloned.1.call-start = ((), (), s32[]{:S(2)}) async-start(), calls=%async_computation.4 | async-start | bytes 1310720 | tf_op jit(solution)/shard_map/reduce_scatter | solution.py:35
  88.1 71.7 %reduce-scatter.6.cloned.1.call-start = ((), (), s32[]{:S(2)}) async-start(), calls=%async_computation.5 | async-start | bytes 1179648 | tf_op jit(solution)/shard_map/reduce_scatter | solution.py:36
  97.0 99.3 %all-reduce.2.cloned.1.call-start = ((), (), s32[]{:S(2)}) async-start(), calls=%async_computation.7 | async-start | bytes 131072 | tf_op jit(solution)/shard_map/psum | solution.py:24
Sparse Core Ops, SparseCore 0:
  57.8 34.6 reduce-scatter.7
  94.8 27.2 reduce-scatter.3
  125.3 34.4 reduce-scatter.5
  162.0 34.2 all-reduce.1
